TPU v7x, 32 devices: a whole 2x2x4 slice. The times are simulated.
32 devices in a mesh: ctx: 16 (over z, x, core), head: 2 (over y).
Axes of the slice: x: 2, y: 2, z: 4, core: 2. Of those that a mesh axis runs over, the one named last changes fastest.
Arguments:
- conv_in: bfloat16 [8192, 2048], P('ctx', 'head'), may hold values from -6 to 6
- conv_weight: float32 [4, 2048], P(None, 'head'), may hold values from -3 to 3
- conv_bias: float32 [2048], P('head'), may hold values from -3 to 3
- qk_weight: bfloat16 [2, 8, 256, 256], P(None, 'head'), may hold values from -0.375 to 0.375
- value_in: bfloat16 [8192, 4096], P('ctx', 'head'), may hold values from -6 to 6
- gate_pre: float32 [2, 8, 8192], P(None, 'head', 'ctx'), may hold values from -6 to 300, as said below
- norm_gain: float32 [4096], P('head'), may hold values from 0.5 to 1.5
- out_weight: bfloat16 [4096, 4096], P('head'), may hold values from -0.125 to 0.125
Outputs:
- layer_out: bfloat16 [8192, 4096], P('ctx', 'head')
Inputs may be any that keep to these rules, and one draw needn't show every extreme that they name: gate_pre[0] holds input-gate preactivations and gate_pre[1] forget-gate preactivations.
All inputs are finite; a program needn't handle non-finite values.
Results may differ from a plain program's by a relative error of at most 0.02.
Values may be sent and summed in bfloat16 or wider, within the bound.
No kernel may reach another device: no remote copies, remote signals or barrier semaphores. Data moves between devices by JAX's collectives and lax.ppermute only.
A program may use at most 192 MiB of HBM per device.

v0:
```python
import jax
import jax.numpy as jnp
from jax import lax
from jax.sharding import PartitionSpec as P

BLOCK = 512


def from_behind(block, axis, distance):
    devices = range(lax.axis_size(axis))
    route = [(i - distance, i) for i in devices if i - distance in devices]
    return lax.ppermute(block, axis, route)


def local_block(carry_state, block_data):
    state_mat, state_max, decay_base = carry_state
    queries, key_rows, values, in_gate, log_forget = block_data
    block_len = in_gate.shape[1]
    cum_decay = jnp.cumsum(log_forget, axis=1)
    row_ids = lax.broadcasted_iota(jnp.int32, (block_len, block_len), 0)
    col_ids = lax.broadcasted_iota(jnp.int32, (block_len, block_len), 1)
    log_weight = jnp.where(
        (row_ids >= col_ids)[None],
        cum_decay[:, :, None] - cum_decay[:, None, :] + in_gate[:, None, :],
        -jnp.inf,
    )
    carry_log = cum_decay + state_max[:, None]
    stabilizer = jnp.maximum(jnp.max(log_weight, axis=2), carry_log)
    scores = jnp.einsum("thd,shd->hts", queries, key_rows, preferred_element_type=jnp.float32)
    weights = (scores * jnp.exp(log_weight - stabilizer[:, :, None])).astype(jnp.bfloat16)
    inner_sum = jnp.einsum("hts,shv->thv", weights, values, preferred_element_type=jnp.float32)
    carried = jnp.einsum(
        "thd,hdv->thv", queries.astype(jnp.float32), state_mat, precision=lax.Precision.HIGHEST
    )
    numerator = inner_sum + jnp.exp(carry_log - stabilizer).T[:, :, None] * carried
    block_decay = cum_decay[:, -1]
    end_log = block_decay[:, None] - cum_decay + in_gate
    new_max = jnp.maximum(state_max + block_decay, jnp.max(end_log, axis=1))
    scaled = (
        key_rows.astype(jnp.float32) * jnp.exp(end_log - new_max[:, None]).T[:, :, None]
    ).astype(jnp.bfloat16)
    update = jnp.einsum("shd,shv->hdv", scaled, values, preferred_element_type=jnp.float32)
    state_mat = jnp.exp(state_max + block_decay - new_max)[:, None, None] * state_mat + update
    outputs = (numerator, stabilizer.T, (cum_decay + decay_base[:, None]).T)
    return ((state_mat, new_max, decay_base + block_decay), outputs)


def body(conv_in, conv_weight, conv_bias, qk_weight, value_in, gate_pre, norm_gain, out_weight):
    tok_rows = conv_in.shape[0]
    head_count = qk_weight.shape[1]
    key_dim = qk_weight.shape[2]
    value_dim = value_in.shape[1] // head_count
    conv_len = conv_weight.shape[0]
    rim_rows = from_behind(conv_in[tok_rows - (conv_len - 1) :], "ctx", 1)
    padded = jnp.concatenate([rim_rows, conv_in], axis=0).astype(jnp.float32)
    conv_pre = conv_bias + conv_weight[0] * padded[0:tok_rows]
    for offset in range(1, conv_len):
        conv_pre = conv_pre + conv_weight[offset] * padded[offset : offset + tok_rows]
    activated = jax.nn.silu(conv_pre).astype(jnp.bfloat16).reshape(tok_rows, head_count, key_dim)
    queries = jnp.einsum(
        "thd,hde->the", activated, qk_weight[0], preferred_element_type=jnp.float32
    ).astype(jnp.bfloat16)
    key_rows = (
        jnp.einsum("thd,hde->the", activated, qk_weight[1], preferred_element_type=jnp.float32)
        * key_dim ** (-0.5)
    ).astype(jnp.bfloat16)
    values = value_in.reshape(tok_rows, head_count, value_dim)
    in_gate = gate_pre[0]
    log_forget = jax.nn.log_sigmoid(gate_pre[1])
    num_blocks = tok_rows // BLOCK
    inputs = (
        queries.reshape(num_blocks, BLOCK, head_count, key_dim),
        key_rows.reshape(num_blocks, BLOCK, head_count, key_dim),
        values.reshape(num_blocks, BLOCK, head_count, value_dim),
        in_gate.reshape(head_count, num_blocks, BLOCK).transpose(1, 0, 2),
        log_forget.reshape(head_count, num_blocks, BLOCK).transpose(1, 0, 2),
    )
    start = (
        jnp.zeros((head_count, key_dim, value_dim), jnp.float32),
        jnp.full((head_count,), -1e30, jnp.float32),
        jnp.zeros((head_count,), jnp.float32),
    )
    summary, outputs = lax.scan(local_block, start, inputs)
    numerator = outputs[0].reshape(tok_rows, head_count, value_dim)
    local_max = outputs[1].reshape(tok_rows, head_count)
    decay_sum = outputs[2].reshape(tok_rows, head_count)
    summary_mat, summary_max, summary_decay = summary
    count = lax.axis_size("ctx")
    pieces = lax.all_to_all(summary_mat[None], "ctx", split_axis=2, concat_axis=0, tiled=True)
    all_max, all_sums = (
        lax.all_gather(summary_max[None], "ctx", axis=0, tiled=True),
        lax.all_gather(summary_decay[None], "ctx", axis=0, tiled=True),
    )
    target_ids = lax.broadcasted_iota(jnp.int32, (count, count, count), 0)
    source_ids = lax.broadcasted_iota(jnp.int32, (count, count, count), 1)
    middle_ids = lax.broadcasted_iota(jnp.int32, (count, count, count), 2)
    inside = ((middle_ids > source_ids) & (middle_ids < target_ids)).astype(jnp.float32)
    between = jnp.einsum("jil,lh->jih", inside, all_sums, precision=lax.Precision.HIGHEST)
    target_two = lax.broadcasted_iota(jnp.int32, (count, count), 0)
    source_two = lax.broadcasted_iota(jnp.int32, (count, count), 1)
    log_mix = jnp.where(
        (source_two < target_two)[:, :, None], all_max[None, :, :] + between, -jnp.inf
    )
    target_max = jnp.maximum(jnp.max(log_mix, axis=1), -1e30)
    mix_weight = jnp.exp(log_mix - target_max[:, None, :])
    prefix = jnp.einsum("jih,ihkv->jhkv", mix_weight, pieces, precision=lax.Precision.HIGHEST)
    returned = lax.all_to_all(prefix, "ctx", split_axis=0, concat_axis=2, tiled=True)
    carry_mat = returned[0]
    carry_max = lax.dynamic_index_in_dim(target_max, lax.axis_index("ctx"), 0, keepdims=False)
    new_max = jnp.maximum(local_max, carry_max[None, :] + decay_sum)
    carried = jnp.einsum(
        "thd,hdv->thv", queries.astype(jnp.float32), carry_mat, precision=lax.Precision.HIGHEST
    )
    numerator = (
        numerator * jnp.exp(local_max - new_max)[:, :, None]
        + jnp.exp(carry_max[None, :] + decay_sum - new_max)[:, :, None] * carried
    )
    scale_inv = lax.rsqrt(jnp.mean(numerator * numerator, axis=2, keepdims=True) + 1e-06)
    normed = (
        (numerator * scale_inv * norm_gain.reshape(head_count, value_dim))
        .astype(jnp.bfloat16)
        .reshape(tok_rows, head_count * value_dim)
    )
    partial_value = jnp.dot(normed, out_weight, preferred_element_type=jnp.float32)
    return lax.psum_scatter(
        partial_value.astype(jnp.bfloat16), "head", scatter_dimension=1, tiled=True
    )


def solution(mesh):
    return jax.shard_map(
        body,
        mesh=mesh,
        in_specs=(
            P("ctx", "head"),
            P(None, "head"),
            P("head"),
            P(None, "head", None, None),
            P("ctx", "head"),
            P(None, "head", "ctx"),
            P("head"),
            P("head", None),
        ),
        out_specs=P("ctx", "head"),
        check_vma=False,
    )
```

profile of v0, /device:TPU:0, one launch (start us, length us, event | category | flops | bytes accessed | tf_op | source)
XLA Modules:
  0.0 259.5 jit_solution(4486996550904070414)
XLA Ops:
  6.5 0.7 slice.50
  7.3 2.4 collective-permute-start
  9.7 0.1 iota_compare_fusion
  9.8 0.7 slice_negate_fusion
  10.5 1.2 reduce-window.6
  11.8 0.2 slice_reduce_fusion
  11.9 0.2 reduce-window.9
  12.1 0.1 add_bitcast_fusion.1
  12.2 0.1 slice.70
  12.3 0.1 copy.68
  12.3 1.2 fusion.3
  13.5 0.9 exponential_bitcast_fusion.2
  14.4 0.8 exponential_bitcast_fusion.1
  15.2 0.9 fusion.50
  16.1 1.2 dynamic-slice.3
  18.0 0.1 bitcast_dynamic-update-slice_fusion
  18.1 0.0 collective-permute-done
  18.1 1.5 maximum_convert_fusion
  19.6 0.0 copy-start.5
  19.6 1.3 multiply_convert_fusion.4
  21.0 0.0 copy-start.4
  21.0 0.4 fusion.22
  21.5 1.9 copy-done.4
  23.3 1.3 add_bitcast_fusion
  24.7 2.7 %copy.52 = f32[1,4,256,512]{3,1,0,2:T(4,128)} copy(f32[1,4,256,512]{3,2,1,0:T(8,128)S(1)} %add_bitcast_fusion) | data formatting | bytes 4194304 | tf_op jit(solution)/shard_map/broadcast_in_dim | solution.py:89
  27.4 7.2 %all-to-all-start = ((f32[1,4,256,512]{3,1,0,2:T(4,128)}), f32[1,4,256,512]{3,1,0,2:T(4,128)S(1)}, u32[]{:S(2)}, u32[]{:S(2)}) async-start(f32[1,4,256,512]{3,1,0,2:T(4,128)} %copy.52), calls=%async_computation | async-start | bytes 4194304 | tf_op jit(solution)/shard_map/all_to_all | solution.py:89
  34.6 62.4 %all-reduce = f32[64]{0:T(128)S(1)} all-reduce(f32[64]{0:T(128)S(1)} %get-tuple-element.52), channel_id=2, replica_groups=mesh['ctx'=16,'head'=2] {'ctx'}, use_global_device_ids=true, to_apply=%add | all-reduce | flops 64 | bytes 512
  96.9 0.1 reshape.137
  97.0 19.8 %all-gather.1 = f32[16,1,4]{2,1,0:T(1,128)S(1)} all-gather(f32[1,1,4]{2,1,0:T(1,128)S(1)} %fusion.45), channel_id=1, replica_groups=mesh['ctx'=16,'head'=2] {'ctx'}, dimensions={0}, use_global_device_ids=true | all-gather | bytes 272 | tf_op jit(solution)/shard_map/all_gather | solution.py:91
  116.8 0.1 copy.48
  116.9 0.7 fusion.51
  117.5 0.1 exponential_bitcast_fusion
  117.7 3.3 %fusion.17 = f32[16,4,16,512]{3,0,2,1:T(8,128)S(1)} fusion(f32[1,4,16,16,512]{4,1,3,2,0:T(4,128)S(1)} %bitcast.132, f32[16,16,4,1]{1,2,0,3:T(4,128)S(1)} %exponential_bitcast_fusion), kind=kOutput, calls=%fused_computation.32 | convolution fusion | flops 100663296 | bytes 4198400 | tf_op jit(solution)/shard_map/jih,ihkv->jhkv/dot_general | solution.py:106
  121.0 2.5 copy.56
  123.5 3.9 %all-to-all-start.1 = ((f32[16,4,16,512]{3,2,1,0:T(8,128)}), f32[16,4,16,512]{3,2,1,0:T(8,128)S(1)}, u32[]{:S(2)}, u32[]{:S(2)}) async-start(f32[16,4,16,512]{3,2,1,0:T(8,128)} %copy.56), calls=%async_computation.1 | async-start | bytes 4194304 | tf_op jit(solution)/shard_map/all_to_all | solution.py:107
  127.4 0.2 reduce-scatter.2.cloned.1.call-start
  127.6 0.1 fusion.39
  127.7 1.8 fusion.23
  129.5 3.8 %fusion.28 = f32[4,512,512]{2,1,0:T(8,128)} fusion(bf16[512,4,256]{2,0,1:T(8,128)(2,1)S(1)} %fusion.23), kind=kOutput, calls=%fused_computation.42 | convolution fusion | flops 3221225472 | bytes 5242880 | tf_op jit(solution)/shard_map/while/body/eval_jaxpr/thd,hdv->thv/dot_general | solution.py:32
  133.3 6.3 %fusion.4 = f32[4,512,512]{1,2,0:T(8,128)} fusion(bf16[64,4,8,512]{3,2,1,0:T(8,128)(2,1)} %bitcast.147, bf16[512,4,256]{2,0,1:T(8,128)(2,1)S(1)} %fusion.23, bf16[512,4,256]{2,0,1:T(8,128)(2,1)} %copy-done.6, f32[4,512]{1,0:T(4,128)S(1)} %get-tuple-element.30, f32[4,512]{1,0:T(4,128)S(1)} %get-tuple-element.32, f32[4,512]{1,0:T(4,128)S(1)} %bitcast.138, ...), kind=kOutput, calls=%fused_computation.11 | convolution fusion | flops 1616904192 | bytes 8675328 | tf_op jit(solution)/shard_map/while/body/eval_jaxpr/hts,shv->thv/dot_general | solution.py:31
  139.6 28.7 %all-to-all-done.1 = f32[16,4,16,512]{3,2,1,0:T(8,128)S(1)} async-done(((f32[16,4,16,512]{3,2,1,0:T(8,128)}), f32[16,4,16,512]{3,2,1,0:T(8,128)S(1)}, u32[]{:S(2)}, u32[]{:S(2)}) %all-to-all-start.1) | async-done | bytes 2097184 | tf_op jit(solution)/shard_map/all_to_all | solution.py:107
  168.3 0.2 copy.57
  168.5 2.0 copy-done
  170.5 6.4 %multiply_reduce_fusion = (f32[512,4]{0,1:T(4,128)S(1)}, f32[512,4,512]{0,2,1:T(8,128)S(1)}) fusion(f32[4,256,512]{2,1,0:T(8,128)S(1)} %bitcast.131, bf16[512,4,256]{2,0,1:T(8,128)(2,1)S(1)} %fusion.23, f32[512,4]{0,1:T(4,128)S(1)} %get-tuple-element.28, f32[512,4]{0,1:T(4,128)S(1)} %get-tuple-element.27, f32[4,512,512]{2,1,0:T(8,128)S(1)} %copy-done, ...), kind=kOutput, calls=%fused_computation.7 | convolution fusion | flops 3228563456 | bytes 15761408 | tf_op jit(solution)/shard_map/thd,hdv->thv/dot_general | solution.py:111
  176.9 0.5 multiply_convert_fusion
  177.4 14.1 %convolution_convert_fusion = bf16[512,4096]{1,0:T(8,128)(2,1)} fusion(bf16[512,2048]{0,1:T(8,128)(2,1)S(1)} %bitcast.133, bf16[2048,4096]{1,0:T(8,128)(2,1)} %param.15), kind=kOutput, calls=%fused_computation | convolution fusion | flops 8592031744 | bytes 23068672 | tf_op jit(solution)/shard_map/dot_general | solution.py:124
  191.5 0.0 reduce-scatter.2.cloned.1.call-update
  191.5 61.1 %reduce-scatter.2.cloned.1.call-done = bf16[512,2048]{1,0:T(8,128)(2,1)} async-done(((bf16[512,4096]{1,0:T(8,128)(2,1)}), bf16[512,2048]{1,0:T(8,128)(2,1)}) %reduce-scatter.2.cloned.1.call-update) | async-done | bytes 2097168 | tf_op jit(solution)/shard_map/reduce_scatter | solution.py:125
  (22 shorter events, 0.1 us)
Async XLA Ops:
  6.5 13.1 %copy-start.3 = (f32[1024]{0:T(1024)S(1)}, f32[1024]{0:T(1024)}, u32[]{:S(2)}) copy-start(f32[1024]{0:T(1024)} %param.10) | copy-start | bytes 12292
  7.3 10.8 %collective-permute-start = (bf16[3,1024]{1,0:T(4,128)(2,1)S(1)}, bf16[3,1024]{1,0:T(4,128)(2,1)S(1)}, u32[]{:S(2)}, u32[]{:S(2)}) collective-permute-start(bf16[3,1024]{1,0:T(4,128)(2,1)S(1)} %slice.50), channel_id=1, source_target_pairs={{0,2},{2,4},{4,6},{6,8},{8,10},{10,12},{12,14},{14,16},{16,18},{18... | collective-permute-start | bytes 18440 | tf_op jit(solution)/shard_map/ppermute | solution.py:12
  19.6 1.4 copy-start.5
  21.0 3.7 %copy-start.1 = (bf16[512,1024]{1,0:T(8,128)(2,1)}, bf16[512,1024]{1,0:T(8,128)(2,1)S(1)}, u32[]{:S(2)}) copy-start(bf16[512,1024]{1,0:T(8,128)(2,1)S(1)} %multiply_convert_fusion.4) | copy-start | bytes 3145732
  21.0 2.4 copy-start.4
  21.5 3.2 %copy-start.6 = (bf16[512,4,256]{2,0,1:T(8,128)(2,1)}, bf16[512,4,256]{2,0,1:T(8,128)(2,1)S(1)}, u32[]{:S(2)}) copy-start(bf16[512,4,256]{2,0,1:T(8,128)(2,1)S(1)} %fusion.22) | copy-start | bytes 3145732
  27.4 90.3 %all-to-all-start = ((f32[1,4,256,512]{3,1,0,2:T(4,128)}), f32[1,4,256,512]{3,1,0,2:T(4,128)S(1)}, u32[]{:S(2)}, u32[]{:S(2)}) async-start(f32[1,4,256,512]{3,1,0,2:T(4,128)} %copy.52), calls=%async_computation | async-start | bytes 4194304 | tf_op jit(solution)/shard_map/all_to_all | solution.py:89
  123.5 4.1 %copy-start.2 = (f32[2048]{0:T(1024)S(1)}, f32[2048]{0:T(1024)}, u32[]{:S(2)}) copy-start(f32[2048]{0:T(1024)} %param.14) | copy-start | bytes 24580
  123.5 44.8 %all-to-all-start.1 = ((f32[16,4,16,512]{3,2,1,0:T(8,128)}), f32[16,4,16,512]{3,2,1,0:T(8,128)S(1)}, u32[]{:S(2)}, u32[]{:S(2)}) async-start(f32[16,4,16,512]{3,2,1,0:T(8,128)} %copy.56), calls=%async_computation.1 | async-start | bytes 4194304 | tf_op jit(solution)/shard_map/all_to_all | solution.py:107
  127.4 125.3 %reduce-scatter.2.cloned.1.call-start = ((), (), s32[]{:S(2)}) async-start(), calls=%async_computation.3 | async-start | bytes 6291456 | tf_op jit(solution)/shard_map/reduce_scatter | solution.py:125
  168.3 2.2 copy-start
Sparse Core Ops, SparseCore 0:
  191.6 60.9 reduce-scatter.1
where the time goes:
time: 260 us; the launch traced here: 259 us
  waiting for transfers between devices  89.8 us (35%)
  blocking collectives  82.1 us (32%)
  matrix products  38.1 us (15%)
  between operations  14.3 us (6%)
  starting transfers between devices  13.6 us (5%)
  local copies, waits for them, and re-layouts  12.7 us (5%)
  other arithmetic  8.78 us (3%)
    unnamed x1, blocking collectives  62.4 us
    reduce_scatter x1, waiting for transfers between devices, body(): lax.psum_scatter(partial_value.astype(jnp.bfloat16), 'head', scatter_dime...  61.1 us
    all_to_all x1, waiting for transfers between devices, body(): lax.all_to_all(prefix, 'ctx', split_axis=0, concat_axis=2, tiled=True)  28.7 us
    all_gather x1, blocking collectives, body(): lax.all_gather(summary_max[None], 'ctx', axis=0, tiled=True)  19.8 us
    dot_general x1, matrix products, body(): jnp.dot(normed, out_weight, preferred_element_type=jnp.float32)  14.1 us
    all_to_all x1, starting transfers between devices, body(): lax.all_to_all(summary_mat[None], 'ctx', split_axis=2, concat_axis=0, til...  7.18 us
    dot_general x1, matrix products, body(): jnp.einsum('thd,hdv->thv', queries.astype(jnp.float32), carry_mat, precis...  6.41 us
    dot_general x1, matrix products, local_block(): jnp.einsum('hts,shv->thv', weights, values, preferred_element_type=jnp.fl...  6.3 us
  transfers between devices with their start and end apart: 4, of which 2 were waited for; matrix products, arithmetic and copies ran while one was open for 8% of the time, Pallas kernels for 0%

commit v1 on v0

v1 whole, which is shorter than its diff:
```python
import functools
import jax
import jax.numpy as jnp
from jax import lax
from jax.experimental import pallas as pl
from jax.experimental.pallas import tpu as pltpu
from jax.sharding import PartitionSpec as P


F32 = jnp.float32
BF16 = jnp.bfloat16
EMPTY = -1e30
TILE = 16
LANES = 128


def dot(a, b, ca, cb):
    return lax.dot_general(a, b, (((ca,), (cb,)), ((), ())), preferred_element_type=F32)


VMEM = pl.BlockSpec(memory_space=pltpu.VMEM)
SMEM = pl.BlockSpec(memory_space=pltpu.SMEM)
ANY = pl.BlockSpec(memory_space=pl.ANY)


def call(kernel, args, out_shape, scratch=(), aliases={}, cost=None, limit=12, specs=None, out=VMEM):
    if specs is None:
        specs = [SMEM if a.dtype == jnp.int32 else VMEM for a in args]
    return pl.pallas_call(
        kernel,
        in_specs=specs,
        out_specs=jax.tree.map(lambda _: out, out_shape),
        scratch_shapes=list(scratch),
        out_shape=out_shape,
        input_output_aliases=aliases,
        cost_estimate=cost,
        compiler_params=pltpu.CompilerParams(vmem_limit_bytes=limit * 2**20),
    )(*args)


def sds(shape, dtype):
    return jax.ShapeDtypeStruct(shape, dtype)


def cost_of(flops, moved):
    return pl.CostEstimate(flops=int(flops), transcendentals=0, bytes_accessed=int(moved))


def window(index, size):
    return pl.ds(pl.multiple_of(index * size, size), size)


def gate_kernel(count, gate_hbm, *rest):
    sources, (line_ref, cols_ref, sums_ref), targets = rest[:count], rest[count : count + 3], rest[count + 3 : -3]
    gate_ref, gate_sem, sems = rest[-3:]
    first = pltpu.make_async_copy(gate_hbm, gate_ref, gate_sem)
    first.start()
    copies = [pltpu.make_async_copy(sources[i], targets[i], sems.at[i]) for i in range(count)]
    for copy in copies:
        copy.start()
    first.wait()
    gates(gate_ref, line_ref, cols_ref, sums_ref)
    for copy in copies:
        copy.wait()


def gates(gate_ref, rows_ref, cols_ref, sums_ref):
    in_gate = gate_ref[0]
    pre = gate_ref[1]
    heads, length = in_gate.shape
    log_forget = -(jnp.maximum(-pre, 0.0) + jnp.log1p(jnp.exp(-jnp.abs(pre))))
    cum = jnp.concatenate([log_forget, in_gate], axis=0)
    lane = lax.broadcasted_iota(jnp.int32, cum.shape, 1)
    step = 1
    while step < length:
        cum = cum + jnp.where(lane >= step, pltpu.roll(cum, step, 1), 0.0)
        step *= 2
    cum = cum[:heads]
    shifted = in_gate - cum
    run = jnp.concatenate([shifted, shifted], axis=0)
    rows_ref[...] = run
    step = 1
    while step < length:
        run = jnp.maximum(run, jnp.where(lane >= step, pltpu.roll(run, step, 1), -jnp.inf))
        step *= 2
    run = run[:heads]
    decay = cum[:, length - 1 :]
    top = run[:, length - 1 :]
    cols_ref[...] = jnp.transpose(jnp.concatenate([run, jnp.exp(shifted - top)], axis=0))
    sums = jnp.concatenate([top + decay, decay], axis=0)
    sums_ref[...] = jnp.broadcast_to(sums, (2 * heads, LANES))


def column(cols_ref, index):
    cols = cols_ref[...]
    lane = lax.broadcasted_iota(jnp.int32, cols.shape, 1)
    return jnp.sum(jnp.where(lane == index, cols, 0.0), axis=1, keepdims=True)


def state_kernel(keep, scale, ids, halo_ref, conv_ref, taps_ref, bias_ref, weight_ref, value_ref, cols_ref,
                 act_ref, key_ref, state_ref, pad):
    half, keys, width = state_ref.shape
    group = ids[0] if keep else 1 - ids[0]
    rows = conv_ref.shape[0]
    taps = taps_ref.shape[0]
    for local in range(half):
        head = group * half + local
        mine = window(head, keys)
        here = slice(local * keys, (local + 1) * keys)
        pad[0:8, :] = halo_ref[TILE - 8 :, mine].astype(F32)
        pad[8:, :] = conv_ref[:, mine].astype(F32)
        total = bias_ref[:, mine]
        for offset in range(taps):
            begin = 8 - (taps - 1) + offset
            total = total + taps_ref[offset : offset + 1, mine] * pad[begin : begin + rows, :]
        act = (total / (1.0 + jnp.exp(-total))).astype(BF16)
        act_ref[:, here] = act
        key_rows = (dot(act, weight_ref[1, head], 1, 0) * scale).astype(BF16)
        key_ref[:, here] = key_rows
        scaled = (key_rows.astype(F32) * column(cols_ref, 2 * half + head)).astype(BF16)
        state_ref[local] = dot(scaled, value_ref[:, window(head, width)], 0, 0).astype(BF16)


def inner_kernel(keep, ids, act_ref, key_ref, weight_ref, value_ref, rows_ref, cols_ref, query_ref, inner_ref, run_ref):
    half = act_ref.shape[1] // weight_ref.shape[2]
    keys = weight_ref.shape[2]
    width = inner_ref.shape[1] // half
    group = ids[0] if keep else 1 - ids[0]
    for local in range(half):
        head = group * half + local
        here = slice(local * keys, (local + 1) * keys)
        queries = dot(act_ref[:, here], weight_ref[0, head], 1, 0).astype(BF16)
        query_ref[:, here] = queries
        scores = dot(queries, key_ref[:, here], 1, 1)
        row = lax.broadcasted_iota(jnp.int32, scores.shape, 0)
        col = lax.broadcasted_iota(jnp.int32, scores.shape, 1)
        run = column(cols_ref, head)
        run_ref[local] = jnp.broadcast_to(run, (run.shape[0], LANES))
        log_weight = rows_ref[pl.ds(head, 1), :] - run
        weights = scores * jnp.exp(jnp.where(row >= col, log_weight, -jnp.inf))
        inner = dot(weights.astype(BF16), value_ref[:, window(head, width)], 1, 0)
        inner_ref[:, local * width : (local + 1) * width] = inner.astype(BF16)


def split_rows(value):
    high = value.astype(BF16).astype(F32)
    rest = value - high
    middle = rest.astype(BF16).astype(F32)
    return [high, middle, rest - middle]


def scalar_tile(values):
    rows = [row for value in values for row in split_rows(value)]
    rows.append(jnp.zeros((TILE - len(rows), LANES), F32))
    return jnp.concatenate(rows, axis=0).astype(BF16)


def join_rows(tile, index):
    tile = tile.astype(F32)
    return tile[3 * index : 3 * index + 1] + tile[3 * index + 1 : 3 * index + 2] + tile[3 * index + 2 : 3 * index + 3]


def wide(row, width):
    return jnp.concatenate([row] * (width // LANES), axis=1)


def place(owner, per, cut, part, span):
    block = lax.div(owner, cut)
    local = lax.div(block, per)
    row = pl.multiple_of(lax.rem(block, per) * part, part)
    lane = pl.multiple_of(lax.rem(owner, cut) * span, LANES)
    return local, row, lane


def chip_kernel(chips, sizes, ids, own_ref, other_ref, own_sums, other_sums, *rest):
    outs, weights = rest[:chips], rest[chips]
    core, chip = ids[0], ids[1]
    half = own_ref.shape[0]
    heads = 2 * half
    part, span = sizes[2], sizes[3]
    first = core == 0
    for local in range(half):
        head = core * half + local
        own_top, own_decay = own_sums[pl.ds(head, 1), :], own_sums[pl.ds(heads + head, 1), :]
        far_top, far_decay = other_sums[pl.ds(head, 1), :], other_sums[pl.ds(heads + head, 1), :]
        own_log = own_top + jnp.where(first, far_decay, 0.0)
        far_log = far_top + jnp.where(first, 0.0, own_decay)
        top = jnp.maximum(own_log, far_log)
        weights[4 * local : 4 * local + 1] = jnp.exp(own_log - top)
        weights[4 * local + 1 : 4 * local + 2] = jnp.exp(far_log - top)
        weights[4 * local + 2 : 4 * local + 3] = top
        weights[4 * local + 3 : 4 * local + 4] = own_decay + far_decay
    for k in range(chips):
        local, row, lane = place(lax.bitwise_xor(chip, k), *sizes)
        mine = weights[pl.ds(4 * local, 1), :]
        its = weights[pl.ds(4 * local + 1, 1), :]
        for b in range(span // LANES):
            lanes = pl.ds(pl.multiple_of(lane + b * LANES, LANES), LANES)
            own = own_ref[local, pl.ds(row, part), lanes].astype(F32)
            far = other_ref[local, pl.ds(row, part), lanes].astype(F32)
            outs[k][b * part : (b + 1) * part, :] = (mine * own + its * far).astype(BF16)
        outs[k][span // LANES * part :, :] = scalar_tile(
            [weights[pl.ds(4 * local + 2, 1), :], weights[pl.ds(4 * local + 3, 1), :]]
        )


def owner_kernel(chips, ids, *rest):
    ins, outs, held, made = rest[:chips], rest[chips : 2 * chips], rest[2 * chips], rest[2 * chips + 1]
    chip = ids[1]
    size = ins[0].shape[0] - TILE
    for k in range(chips):
        held[k] = ins[k][...]
    total = jnp.zeros((size, LANES), F32)
    top = jnp.full((1, LANES), EMPTY, F32)
    for source in range(chips):
        slot = lax.bitwise_xor(chip, source)
        made[slot, 0:size] = total.astype(BF16)
        made[slot, size:] = scalar_tile([top])
        if source < chips - 1:
            tile = held[slot, size:]
            new, decay = join_rows(tile, 0), join_rows(tile, 1)
            next_top = jnp.maximum(top + decay, new)
            old_weight = jnp.exp(top + decay - next_top)
            new_weight = jnp.exp(new - next_top)
            total = old_weight * total + new_weight * held[slot, 0:size].astype(F32)
            top = next_top
    for k in range(chips):
        outs[k][...] = made[k]


def incoming_kernel(chips, sizes, ids, *rest):
    ins = rest[:chips]
    own_ref, other_ref, own_sums, other_sums, keep_ref, send_ref, keep_top, send_top, tops = rest[chips:]
    core, chip = ids[0], ids[1]
    half = own_ref.shape[0]
    heads = 2 * half
    part, span = sizes[2], sizes[3]
    first = core == 0
    for k in range(chips):
        local, row, lane = place(lax.bitwise_xor(chip, k), *sizes)
        head = core * half + local
        top = join_rows(ins[k][span // LANES * part :, :], 0)
        tops[pl.ds(local, 1), :] = top
        near_top = jnp.where(first, own_sums[pl.ds(head, 1), :], other_sums[pl.ds(head, 1), :])
        near_decay = jnp.where(first, own_sums[pl.ds(heads + head, 1), :], other_sums[pl.ds(heads + head, 1), :])
        next_top = jnp.maximum(top + near_decay, near_top)
        old_weight = jnp.exp(top + near_decay - next_top)
        new_weight = jnp.exp(near_top - next_top)
        tops[pl.ds(4 + local, 1), :] = next_top
        for b in range(span // LANES):
            lanes = pl.ds(pl.multiple_of(lane + b * LANES, LANES), LANES)
            raw = ins[k][b * part : (b + 1) * part, :].astype(F32)
            own = own_ref[local, pl.ds(row, part), lanes].astype(F32)
            far = other_ref[local, pl.ds(row, part), lanes].astype(F32)
            after = old_weight * raw + new_weight * jnp.where(first, own, far)
            keep_ref[local, pl.ds(row, part), lanes] = jnp.where(first, raw, after).astype(BF16)
            send_ref[local, pl.ds(row, part), lanes] = jnp.where(first, after, raw).astype(BF16)
    before, after = tops[0:4], tops[4:8]
    keep_top[0:4] = jnp.where(first, before, after)
    keep_top[4:8] = before
    send_top[0:4] = jnp.where(first, after, before)
    send_top[4:8] = before


def norm_kernel(keep, sides, ids, *rest):
    if keep:
        query_ref, inner_ref, carry_ref, top_ref, run_ref, gain_ref, weight_ref, out_ref, chunk_ref = rest
    else:
        query_ref, inner_ref, carry_ref, top_ref, run_ref, gain_ref, weight_ref, begun_ref, out_ref, chunk_ref = rest
    half, keys, width = carry_ref.shape
    group = ids[0] if keep else 1 - ids[0]
    size = chunk_ref.shape[1]
    lanes = first_lanes(1, sides, ids, weight_ref, 0, size)
    total = None
    for local in range(half):
        head = group * half + local
        here = slice(local * width, (local + 1) * width)
        carried = dot(query_ref[:, local * keys : (local + 1) * keys], carry_ref[local], 1, 0)
        run = run_ref[local]
        old = top_ref[local : local + 1, :]
        top = jnp.maximum(run, old)
        numerator = wide(jnp.exp(run - top), width) * inner_ref[:, here].astype(F32)
        numerator = numerator + wide(jnp.exp(old - top), width) * carried
        scale = lax.rsqrt(jnp.mean(numerator * numerator, axis=1, keepdims=True) + 1e-06)
        normed = (numerator * scale * gain_ref[:, window(head, width)]).astype(BF16)
        out_ref[:, here] = normed
        part = dot(normed, weight_ref[window(head, width), lanes], 1, 0)
        total = part if total is None else total + part
    if keep:
        chunk_ref[...] = total
    else:
        chunk_ref[...] = (begun_ref[...] + total).astype(BF16)


def first_lanes(distance, sides, ids, weight_ref, start, size):
    side = lax.rem(ids[2] + distance, sides)
    return pl.ds(pl.multiple_of(side * (weight_ref.shape[1] // sides) + start, LANES), size)


def project_kernel(distance, sides, start, block, ids, near_ref, far_ref, weight_ref, out_ref):
    depth = near_ref.shape[1]
    for i in range(out_ref.shape[1] // block):
        lanes = first_lanes(distance, sides, ids, weight_ref, start + i * block, block)
        total = dot(near_ref[...], weight_ref[window(ids[0], depth), lanes], 1, 0)
        total = total + dot(far_ref[...], weight_ref[window(1 - ids[0], depth), lanes], 1, 0)
        out_ref[:, i * block : (i + 1) * block] = total.astype(BF16)


def add_kernel(start, parts, own_ref, *rest):
    total_ref, made, sem = rest[-3:]
    size = made.shape[1]
    total = own_ref[:, start : start + size].astype(F32)
    for part in rest[:parts]:
        total = total + part[...].astype(F32)
    made[...] = total.astype(BF16)
    copy = pltpu.make_async_copy(made, total_ref.at[:, start : start + size], sem)
    copy.start()
    copy.wait()


def body(conv_in, conv_weight, conv_bias, qk_weight, value_in, gate_pre, norm_gain, out_weight):
    rows = conv_in.shape[0]
    heads, keys = qk_weight.shape[1], qk_weight.shape[2]
    width = value_in.shape[1] // heads
    columns = out_weight.shape[1]
    half = heads // 2
    count = lax.axis_size("ctx")
    chips = count // 2
    cut = max(1, TILE * chips // (half * keys))
    part = half * keys * cut // chips
    sizes = (keys // part, cut, part, width // cut)
    sides = lax.axis_size("head")
    me = lax.axis_index("ctx")
    ids = jnp.stack([lax.rem(me, 2), lax.div(me, 2), lax.axis_index("head")]).astype(jnp.int32)

    swap = [(i, i ^ 1) for i in range(count)]

    def spread(made):
        came = {0: made[0]}
        for k in sorted(range(1, chips), key=lambda k: -(k & -2)):
            came[k] = lax.ppermute(made[k], "ctx", [(i, i ^ (2 * k)) for i in range(count)])
        return [came[k] for k in range(chips)]

    halo = lax.ppermute(conv_in[rows - TILE :], "ctx", [(i, i + 1) for i in range(count - 1)])
    sources = [conv_in, conv_weight, conv_bias.reshape(1, -1), qk_weight, value_in, norm_gain.reshape(1, -1)]
    line, cols, sums, conv, taps, bias, qk, values, gain = call(
        functools.partial(gate_kernel, len(sources)),
        [gate_pre, *sources],
        (sds((2 * heads, rows), F32), sds((rows, 2 * heads), F32), sds((2 * heads, LANES), F32))
        + tuple(sds(a.shape, a.dtype) for a in sources),
        [pltpu.VMEM(gate_pre.shape, F32), pltpu.SemaphoreType.DMA, pltpu.SemaphoreType.DMA((len(sources),))],
        specs=[ANY] * (1 + len(sources)),
    )
    far_sums = lax.ppermute(sums, "ctx", swap)

    def state_of(keep):
        return call(
            functools.partial(state_kernel, keep, keys ** -0.5),
            [ids, halo, conv, taps, bias, qk, values, cols],
            (sds((rows, half * keys), BF16), sds((rows, half * keys), BF16), sds((half, keys, width), BF16)),
            [pltpu.VMEM((rows + 8, keys), F32)],
        )

    def inner_of(keep, act, key_rows):
        return call(
            functools.partial(inner_kernel, keep),
            [ids, act, key_rows, qk, values, line, cols],
            (sds((rows, half * keys), BF16), sds((rows, half * width), BF16), sds((half, rows, LANES), F32)),
            cost=cost_of(2 * rows * half * (keys * keys + rows * keys + rows * width), 4e6),
        )

    send_act, send_keys, send_state = state_of(False)
    other_state = lax.ppermute(send_state, "ctx", swap)
    keep_act, keep_keys, own_state = state_of(True)

    piece = sds((width // cut // LANES * part + TILE, LANES), BF16)
    pieces = call(
        functools.partial(chip_kernel, chips, sizes),
        [ids, own_state, other_state, sums, far_sums],
        (piece,) * chips,
        [pltpu.VMEM((4 * half, LANES), F32)],
    )
    got = spread(pieces)
    send_act, send_keys, _ = lax.optimization_barrier((send_act, send_keys, pieces[0]))
    send_queries, send_inner, send_run = inner_of(False, send_act, send_keys)
    got[0], send_inner = lax.optimization_barrier((got[0], send_inner))

    made = call(
        functools.partial(owner_kernel, chips),
        [ids, *got],
        (piece,) * chips,
        [pltpu.VMEM((chips,) + piece.shape, BF16)] * 2,
    )
    back = spread(made)
    keep_act, keep_keys, _ = lax.optimization_barrier((keep_act, keep_keys, made[0]))
    keep_queries, keep_inner, keep_run = inner_of(True, keep_act, keep_keys)
    back[0], keep_inner = lax.optimization_barrier((back[0], keep_inner))

    state_shape = sds((half, keys, width), BF16)
    keep_carry, send_carry, keep_top, send_top = call(
        functools.partial(incoming_kernel, chips, sizes),
        [ids, *back, own_state, other_state, sums, far_sums],
        (state_shape, state_shape, sds((8, LANES), F32), sds((8, LANES), F32)),
        [pltpu.VMEM((8, LANES), F32)],
    )
    far_carry = lax.ppermute(send_carry, "ctx", swap)
    far_top = lax.ppermute(send_top, "ctx", swap)

    block = 256
    near, begun = call(
        functools.partial(norm_kernel, True, sides),
        [ids, keep_queries, keep_inner, keep_carry, keep_top, keep_run, gain, out_weight],
        (sds((rows, half * width), BF16), sds((rows, block), F32)),
    )
    far, first = call(
        functools.partial(norm_kernel, False, sides),
        [ids, send_queries, send_inner, far_carry, far_top, send_run, gain, out_weight, begun],
        (sds((rows, half * width), BF16), sds((rows, block), BF16)),
    )

    out_columns = columns // sides

    def project(distance, start, size):
        return call(
            functools.partial(project_kernel, distance, sides, start, block),
            [ids, near, far, out_weight],
            sds((rows, size), BF16),
            cost=cost_of(4 * rows * half * width * size, 4 * half * width * size),
        )

    blocks = out_columns // block
    cuts = [0, 1, 1 + (blocks - 2) // 2, blocks - 1, blocks]
    chunks = [(low * block, (high - low) * block) for low, high in zip(cuts, cuts[1:])]
    arrived = {}
    for index in range(len(chunks) * (sides - 1)):
        start, size = chunks[index // (sides - 1)]
        distance = 1 + index % (sides - 1)
        value = first
        if index > 0:
            value = project(distance, start, size)
        came = lax.ppermute(value, "head", [(i, (i + distance) % sides) for i in range(sides)])
        arrived.setdefault((start, size), []).append(came)
    own = project(0, 0, out_columns)
    total = []
    for (start, size), parts in arrived.items():
        total = [
            call(
                functools.partial(add_kernel, start, len(parts)),
                [own, *parts, *total],
                sds((rows, out_columns), BF16),
                [pltpu.VMEM((rows, size), BF16), pltpu.SemaphoreType.DMA],
                aliases={1 + len(parts): 0} if total else {},
                specs=[VMEM] * (1 + len(parts)) + [ANY] * len(total),
                out=ANY,
            )
        ]
    return total[0]


def solution(mesh):
    return jax.shard_map(
        body,
        mesh=mesh,
        in_specs=(
            P("ctx", "head"),
            P(None, "head"),
            P("head"),
            P(None, "head", None, None),
            P("ctx", "head"),
            P(None, "head", "ctx"),
            P("head"),
            P("head", None),
        ),
        out_specs=P("ctx", "head"),
        check_vma=False,
    )
```

time: 260 us -> 117 us (0.45)
  blocking collectives: 82.1 us -> 0 us
  waiting for transfers between devices: 89.8 us -> 43.1 us
  matrix products: 38.1 us -> 0 us
  Pallas kernels: 0 us -> 31.4 us
  starting transfers between devices: 13.6 us -> 33.5 us
  between operations: 14.3 us -> 0.41 us
  other arithmetic: 8.78 us -> 0.08 us
  local copies, waits for them, and re-layouts: 12.7 us -> 7.62 us
    unnamed x1 -> x0, blocking collectives: 62.4 us -> none
    reduce_scatter x1 -> x0, waiting for transfers between devices: 61.1 us -> none  [body(): lax.psum_scatter(partial_value.astype(jnp.bfloat16), 'head', scatter_dime...]
    ppermute x1 -> x23, waiting for transfers between devices: 0.01 us -> 43.1 us  [the longest x4 34.5 us: body(): lax.ppermute(value, 'head', [(i, (i + distance) % sides) for i in range(s...]
    dot_general x9 -> x0, matrix products: 38.1 us -> none  [the longest x1 14.1 us: body(): jnp.dot(normed, out_weight, preferred_element_type=jnp.float32)]
    pallas_call x0 -> x18, Pallas kernels: none -> 31.4 us  [call(): pl.pallas_call(kernel, in_specs=specs, out_specs=jax.tree.map(lambda _: o...]
    ppermute x1 -> x23, starting transfers between devices: 2.38 us -> 33.5 us  [the longest x14 23.6 us: spread(): lax.ppermute(made[k], 'ctx', [(i, i ^ 2 * k) for i in range(count)])]
    all_to_all x2 -> x0, waiting for transfers between devices: 28.7 us -> none  [the longest x1 28.7 us: body(): lax.all_to_all(prefix, 'ctx', split_axis=0, concat_axis=2, tiled=True)]
    all_gather x1 -> x0, blocking collectives: 19.8 us -> none  [body(): lax.all_gather(summary_max[None], 'ctx', axis=0, tiled=True)]
  transfers between devices with their start and end apart: 4 -> 23, of which waited for: 2 -> 4; matrix products, arithmetic and copies ran while one was open for 8% -> 0% of each run, Pallas kernels for 0% -> 18%
where the time goes in v1:
time: 117 us; the launch traced here: 116 us
  waiting for transfers between devices  43.1 us (37%)
  starting transfers between devices  33.5 us (29%)
  Pallas kernels  31.4 us (27%)
  local copies, waits for them, and re-layouts  7.62 us (7%)
    ppermute x4, waiting for transfers between devices, body(): lax.ppermute(value, 'head', [(i, (i + distance) % sides) for i in range(s...  34.5 us
    pallas_call x18, Pallas kernels, call(): pl.pallas_call(kernel, in_specs=specs, out_specs=jax.tree.map(lambda _: o...  31.4 us
    ppermute x14, starting transfers between devices, spread(): lax.ppermute(made[k], 'ctx', [(i, i ^ 2 * k) for i in range(count)])  23.6 us
    ppermute x14, waiting for transfers between devices, spread(): lax.ppermute(made[k], 'ctx', [(i, i ^ 2 * k) for i in range(count)])  8.67 us
    unnamed x16, local copies, waits for them, and re-layouts  6.86 us
    ppermute x4, starting transfers between devices, body(): lax.ppermute(value, 'head', [(i, (i + distance) % sides) for i in range(s...  4.24 us
    ppermute x1, starting transfers between devices, body(): other_state = lax.ppermute(send_state, 'ctx', swap)  2.66 us
    ppermute x1, starting transfers between devices, body(): lax.ppermute(conv_in[rows - TILE:], 'ctx', [(i, i + 1) for i in range(cou...  2.39 us
  transfers between devices with their start and end apart: 23, of which 4 were waited for; matrix products, arithmetic and copies ran while one was open for 0% of the time, Pallas kernels for 18%

profile of v1, /device:TPU:0, one launch (start us, length us, event | category | flops | bytes accessed | tf_op | source)
XLA Modules:
  0.0 116.2 jit_solution(11145828797668310694)
XLA Ops:
  0.0 0.8 slice.3
  0.8 2.4 %collective-permute-start = (bf16[16,1024]{1,0:T(8,128)(2,1)S(1)}, bf16[16,1024]{1,0:T(8,128)(2,1)S(1)}, u32[]{:S(2)}, u32[]{:S(2)}) collective-permute-start(bf16[16,1024]{1,0:T(8,128)(2,1)S(1)} %slice.3), channel_id=1, source_target_pairs={{0,2},{2,4},{4,6},{6,8},{8,10},{10,12},{12,14},{14,16},{16,18},{18... | collective-permute-start | bytes 98312 | tf_op jit(solution)/shard_map/ppermute | solution.py:344
  3.2 1.6 %copy-done.1 = bf16[512,2048]{1,0:T(8,128)(2,1)S(1)} copy-done((bf16[512,2048]{1,0:T(8,128)(2,1)S(1)}, bf16[512,2048]{1,0:T(8,128)(2,1)}, u32[]{:S(2)}) %copy-start.1) | copy-done | bytes 2097176
  4.8 1.2 %copy-done.2 = bf16[512,1024]{1,0:T(8,128)(2,1)S(1)} copy-done((bf16[512,1024]{1,0:T(8,128)(2,1)S(1)}, bf16[512,1024]{1,0:T(8,128)(2,1)}, u32[]{:S(2)}) %copy-start.2) | copy-done | bytes 1048600
  6.1 1.2 %copy-done.3 = bf16[2,4,256,256]{3,2,1,0:T(8,128)(2,1)S(1)} copy-done((bf16[2,4,256,256]{3,2,1,0:T(8,128)(2,1)S(1)}, bf16[2,4,256,256]{3,2,1,0:T(8,128)(2,1)}, u32[]{:S(2)}) %copy-start.3) | copy-done | bytes 1048600
  7.3 0.7 copy-done.4
  8.0 0.7 copy-done.5
  8.7 0.7 copy-done.6
  9.4 0.7 copy-done.7
  10.1 1.6 %shard_map.82 = (f32[8,512]{1,0:T(8,128)S(1)}, f32[512,8]{1,0:T(8,128)S(1)}, f32[8,128]{1,0:T(8,128)S(1)}, bf16[512,1024]{1,0:T(8,128)(2,1)S(1)}, f32[4,1024]{1,...) custom-call(f32[2,4,512]{2,1,0:T(4,128)S(1)} %copy-done.4, ...), custom_call_target="tpu_custom_call" | custom-call | tf_op jit(solution)/shard_map/pallas_call | solution.py:29
  11.8 2.3 %shard_map.84 = (bf16[512,512]{1,0:T(8,128)(2,1)S(1)}, bf16[512,512]{1,0:T(8,128)(2,1)S(1)}, bf16[2,256,512]{2,1,0:T(8,128)(2,1)S(1)}) custom-call(s32[3]{0:T(128)S(1)} %pad_add_fusion.ids, bf16[16,1024]{1,0:T(8,128)(2,1)S(1)} %collective-permute-done.halo_ref, bf16[512,1024]{1,0:T(8,128)(2,1)S(1)} %get-tuple-element.58.conv_ref, ...), custom_call_target="tpu_custom_call" | custom-call | tf_op jit(solution)/shard_map/pallas_call | solution.py:29
  14.1 2.7 %collective-permute-start.1 = (bf16[2,256,512]{2,1,0:T(8,128)(2,1)S(1)}, bf16[2,256,512]{2,1,0:T(8,128)(2,1)S(1)}, u32[]{:S(2)}, u32[]{:S(2)}) collective-permute-start(bf16[2,256,512]{2,1,0:T(8,128)(2,1)S(1)} %get-tuple-element.67), channel_id=1, source_target_pairs={{0,2},{2,0},{4,6},{6,4},{8,10},{10,8},{12,14},{14,12},{16,18},{18,... | collective-permute-start | bytes 1572872 | tf_op jit(solution)/shard_map/ppermute | solution.py:373
  16.8 2.3 %shard_map.83 = (bf16[512,512]{1,0:T(8,128)(2,1)S(1)}, bf16[512,512]{1,0:T(8,128)(2,1)S(1)}, bf16[2,256,512]{2,1,0:T(8,128)(2,1)S(1)}) custom-call(s32[3]{0:T(128)S(1)} %pad_add_fusion.ids, bf16[16,1024]{1,0:T(8,128)(2,1)S(1)} %collective-permute-done.halo_ref, bf16[512,1024]{1,0:T(8,128)(2,1)S(1)} %get-tuple-element.58.conv_ref, ...), custom_call_target="tpu_custom_call" | custom-call | tf_op jit(solution)/shard_map/pallas_call | solution.py:29
  19.1 0.8 shard_map.85
  19.9 1.6 %collective-permute-start.3 = (bf16[272,128]{1,0:T(8,128)(2,1)S(1)}, bf16[272,128]{1,0:T(8,128)(2,1)S(1)}, u32[]{:S(2)}, u32[]{:S(2)}) collective-permute-start(bf16[272,128]{1,0:T(8,128)(2,1)S(1)} %get-tuple-element.77), channel_id=1, source_target_pairs={{0,4},{2,6},{4,0},{6,2},{8,12},{10,14},{12,8},{14,10},{16,20},{18,... | collective-permute-start | bytes 208904 | tf_op jit(solution)/shard_map/ppermute | solution.py:341
  21.5 1.6 %collective-permute-start.4 = (bf16[272,128]{1,0:T(8,128)(2,1)S(1)}, bf16[272,128]{1,0:T(8,128)(2,1)S(1)}, u32[]{:S(2)}, u32[]{:S(2)}) collective-permute-start(bf16[272,128]{1,0:T(8,128)(2,1)S(1)} %get-tuple-element.78), channel_id=1, source_target_pairs={{0,8},{2,10},{4,12},{6,14},{8,0},{10,2},{12,4},{14,6},{16,24},{18,... | collective-permute-start | bytes 208904 | tf_op jit(solution)/shard_map/ppermute | solution.py:341
  23.5 2.6 %collective-permute-start.6 = (bf16[272,128]{1,0:T(8,128)(2,1)S(1)}, bf16[272,128]{1,0:T(8,128)(2,1)S(1)}, u32[]{:S(2)}, u32[]{:S(2)}) collective-permute-start(bf16[272,128]{1,0:T(8,128)(2,1)S(1)} %get-tuple-element.80), channel_id=1, source_target_pairs={{0,16},{2,18},{4,20},{6,22},{8,24},{10,26},{12,28},{14,30},{16,0},... | collective-permute-start | bytes 208904 | tf_op jit(solution)/shard_map/ppermute | solution.py:341
  26.0 1.3 %collective-permute-start.7 = (bf16[272,128]{1,0:T(8,128)(2,1)S(1)}, bf16[272,128]{1,0:T(8,128)(2,1)S(1)}, u32[]{:S(2)}, u32[]{:S(2)}) collective-permute-start(bf16[272,128]{1,0:T(8,128)(2,1)S(1)} %get-tuple-element.81), channel_id=1, source_target_pairs={{0,20},{2,22},{4,16},{6,18},{8,28},{10,30},{12,24},{14,26},{16,4},... | collective-permute-start | bytes 208904 | tf_op jit(solution)/shard_map/ppermute | solution.py:341
  27.4 2.4 %collective-permute-start.8 = (bf16[272,128]{1,0:T(8,128)(2,1)S(1)}, bf16[272,128]{1,0:T(8,128)(2,1)S(1)}, u32[]{:S(2)}, u32[]{:S(2)}) collective-permute-start(bf16[272,128]{1,0:T(8,128)(2,1)S(1)} %get-tuple-element.82), channel_id=1, source_target_pairs={{0,24},{2,26},{4,28},{6,30},{8,16},{10,18},{12,20},{14,22},{16,8},... | collective-permute-start | bytes 208904 | tf_op jit(solution)/shard_map/ppermute | solution.py:341
  29.7 1.4 %collective-permute-start.9 = (bf16[272,128]{1,0:T(8,128)(2,1)S(1)}, bf16[272,128]{1,0:T(8,128)(2,1)S(1)}, u32[]{:S(2)}, u32[]{:S(2)}) collective-permute-start(bf16[272,128]{1,0:T(8,128)(2,1)S(1)} %get-tuple-element.83), channel_id=1, source_target_pairs={{0,28},{2,30},{4,24},{6,26},{8,20},{10,22},{12,16},{14,18},{16,12}... | collective-permute-start | bytes 208904 | tf_op jit(solution)/shard_map/ppermute | solution.py:341
  31.1 1.8 %shard_map.86 = (bf16[512,512]{1,0:T(8,128)(2,1)S(1)}, bf16[512,1024]{1,0:T(8,128)(2,1)S(1)}, f32[2,512,128]{2,1,0:T(8,128)S(1)}) custom-call(s32[3]{0:T(128)S(1)} %pad_add_fusion.ids, bf16[512,512]{1,0:T(8,128)(2,1)S(1)} %get-tuple-element.72.act_ref, bf16[512,512]{1,0:T(8,128)(2,1)S(1)} %get-tuple-element.73.key_ref, ...), custom_call_target="tpu_custom_call" | custom-call | flops 939524096 | bytes 4000000 | tf_op jit(solution)/shard_map/pallas_call | solution.py:29
  32.9 4.4 %collective-permute-done.7.rest_5_ = bf16[272,128]{1,0:T(8,128)(2,1)S(1)} collective-permute-done((bf16[272,128]{1,0:T(8,128)(2,1)S(1)}, bf16[272,128]{1,0:T(8,128)(2,1)S(1)}, u32[]{:S(2)}, u32[]{:S(2)}) %collective-permute-start.7) | collective-permute-done | bytes 69664 | tf_op jit(solution)/shard_map/ppermute | solution.py:341
  37.3 0.8 shard_map.87
  38.1 1.3 %collective-permute-start.10 = (bf16[272,128]{1,0:T(8,128)(2,1)S(1)}, bf16[272,128]{1,0:T(8,128)(2,1)S(1)}, u32[]{:S(2)}, u32[]{:S(2)}) collective-permute-start(bf16[272,128]{1,0:T(8,128)(2,1)S(1)} %get-tuple-element.91), channel_id=1, source_target_pairs={{0,4},{2,6},{4,0},{6,2},{8,12},{10,14},{12,8},{14,10},{16,20},{18,... | collective-permute-start | bytes 208904 | tf_op jit(solution)/shard_map/ppermute | solution.py:341
  39.4 3.1 %collective-permute-start.11 = (bf16[272,128]{1,0:T(8,128)(2,1)S(1)}, bf16[272,128]{1,0:T(8,128)(2,1)S(1)}, u32[]{:S(2)}, u32[]{:S(2)}) collective-permute-start(bf16[272,128]{1,0:T(8,128)(2,1)S(1)} %get-tuple-element.92), channel_id=1, source_target_pairs={{0,8},{2,10},{4,12},{6,14},{8,0},{10,2},{12,4},{14,6},{16,24},{18,... | collective-permute-start | bytes 208904 | tf_op jit(solution)/shard_map/ppermute | solution.py:341
  42.9 2.8 %collective-permute-start.13 = (bf16[272,128]{1,0:T(8,128)(2,1)S(1)}, bf16[272,128]{1,0:T(8,128)(2,1)S(1)}, u32[]{:S(2)}, u32[]{:S(2)}) collective-permute-start(bf16[272,128]{1,0:T(8,128)(2,1)S(1)} %get-tuple-element.94), channel_id=1, source_target_pairs={{0,16},{2,18},{4,20},{6,22},{8,24},{10,26},{12,28},{14,30},{16,0},... | collective-permute-start | bytes 208904 | tf_op jit(solution)/shard_map/ppermute | solution.py:341
  45.7 0.7 collective-permute-start.14
  46.4 2.4 %collective-permute-start.15 = (bf16[272,128]{1,0:T(8,128)(2,1)S(1)}, bf16[272,128]{1,0:T(8,128)(2,1)S(1)}, u32[]{:S(2)}, u32[]{:S(2)}) collective-permute-start(bf16[272,128]{1,0:T(8,128)(2,1)S(1)} %get-tuple-element.96), channel_id=1, source_target_pairs={{0,24},{2,26},{4,28},{6,30},{8,16},{10,18},{12,20},{14,22},{16,8},... | collective-permute-start | bytes 208904 | tf_op jit(solution)/shard_map/ppermute | solution.py:341
  48.7 1.8 %collective-permute-start.16 = (bf16[272,128]{1,0:T(8,128)(2,1)S(1)}, bf16[272,128]{1,0:T(8,128)(2,1)S(1)}, u32[]{:S(2)}, u32[]{:S(2)}) collective-permute-start(bf16[272,128]{1,0:T(8,128)(2,1)S(1)} %get-tuple-element.97), channel_id=1, source_target_pairs={{0,28},{2,30},{4,24},{6,26},{8,20},{10,22},{12,16},{14,18},{16,12}... | collective-permute-start | bytes 208904 | tf_op jit(solution)/shard_map/ppermute | solution.py:341
  50.5 1.8 %shard_map.88 = (bf16[512,512]{1,0:T(8,128)(2,1)S(1)}, bf16[512,1024]{1,0:T(8,128)(2,1)S(1)}, f32[2,512,128]{2,1,0:T(8,128)S(1)}) custom-call(s32[3]{0:T(128)S(1)} %pad_add_fusion.ids, bf16[512,512]{1,0:T(8,128)(2,1)S(1)} %get-tuple-element.85.act_ref, bf16[512,512]{1,0:T(8,128)(2,1)S(1)} %get-tuple-element.86.key_ref, ...), custom_call_target="tpu_custom_call" | custom-call | flops 939524096 | bytes 4000000 | tf_op jit(solution)/shard_map/pallas_call | solution.py:29
  52.3 1.0 collective-permute-done.13.rest_4_
  53.3 3.3 %collective-permute-done.14.rest_5_ = bf16[272,128]{1,0:T(8,128)(2,1)S(1)} collective-permute-done((bf16[272,128]{1,0:T(8,128)(2,1)S(1)}, bf16[272,128]{1,0:T(8,128)(2,1)S(1)}, u32[]{:S(2)}, u32[]{:S(2)}) %collective-permute-start.14) | collective-permute-done | bytes 69664 | tf_op jit(solution)/shard_map/ppermute | solution.py:341
  56.6 1.0 shard_map.89
  57.6 0.5 collective-permute-start.18
  58.1 2.0 %shard_map.90 = (bf16[512,1024]{1,0:T(8,128)(2,1)S(1)}, f32[512,256]{1,0:T(8,128)S(1)}) custom-call(s32[3]{0:T(128)S(1)} %pad_add_fusion.ids, bf16[512,512]{1,0:T(8,128)(2,1)S(1)} %get-tuple-element.87.rest_0_, bf16[512,1024]{1,0:T(8,128)(2,1)S(1)} %get-tuple-element.89.rest_1_, bf16[2,256,512]{2,1,0:T(8,128)(2,1)S(1)} %get-tuple-element.98.rest_2_, ...), custom_call_target="tpu_custom_call" | custom-call | tf_op jit(solution)/shard_map/pallas_call | solution.py:29
  60.1 2.0 %shard_map.91 = (bf16[512,1024]{1,0:T(8,128)(2,1)S(1)}, bf16[512,256]{1,0:T(8,128)(2,1)S(1)}) custom-call(s32[3]{0:T(128)S(1)} %pad_add_fusion.ids, bf16[512,512]{1,0:T(8,128)(2,1)S(1)} %get-tuple-element.103.rest_0_, bf16[512,1024]{1,0:T(8,128)(2,1)S(1)} %get-tuple-element.104.rest_1_, bf16[2,256,512]{2,1,0:T(8,128)(2,1)S(1)} %collective-permute-done.17.rest_2_, ...), custom_call_target="tpu_custom_call" | custom-call | tf_op jit(solution)/shard_map/pallas_call | solution.py:29
  62.1 2.4 %shard_map.95 = bf16[512,768]{1,0:T(8,128)(2,1)S(1)} custom-call(s32[3]{0:T(128)S(1)} %pad_add_fusion.ids, bf16[512,1024]{1,0:T(8,128)(2,1)S(1)} %get-tuple-element.102.near_ref, bf16[512,1024]{1,0:T(8,128)(2,1)S(1)} %get-tuple-element.109.far_ref, bf16[2048,4096]{1,0:T(8,128)(2,1)S(1)} %copy-done), custom_call_target="tpu_custom_call" | custom-call | flops 1610612736 | bytes 3145728 | tf_op jit(solution)/shard_map/pallas_call | solution.py:29
  64.5 1.6 %collective-permute-start.21 = (bf16[512,768]{1,0:T(8,128)(2,1)S(1)}, bf16[512,768]{1,0:T(8,128)(2,1)S(1)}, u32[]{:S(2)}, u32[]{:S(2)}) collective-permute-start(bf16[512,768]{1,0:T(8,128)(2,1)S(1)} %shard_map.95), channel_id=1, source_target_pairs={{0,1},{1,0},{2,3},{3,2},{4,5},{5,4},{6,7},{7,6},{8,9},{9,8},{10,11... | collective-permute-start | bytes 2359304 | tf_op jit(solution)/shard_map/ppermute | solution.py:441
  66.1 2.6 %shard_map.94 = bf16[512,768]{1,0:T(8,128)(2,1)S(1)} custom-call(s32[3]{0:T(128)S(1)} %pad_add_fusion.ids, bf16[512,1024]{1,0:T(8,128)(2,1)S(1)} %get-tuple-element.102.near_ref, bf16[512,1024]{1,0:T(8,128)(2,1)S(1)} %get-tuple-element.109.far_ref, bf16[2048,4096]{1,0:T(8,128)(2,1)S(1)} %copy-done), custom_call_target="tpu_custom_call" | custom-call | flops 1610612736 | bytes 3145728 | tf_op jit(solution)/shard_map/pallas_call | solution.py:29
  68.7 0.5 collective-permute-start.20
  69.3 1.3 %shard_map.93 = bf16[512,256]{1,0:T(8,128)(2,1)S(1)} custom-call(s32[3]{0:T(128)S(1)} %pad_add_fusion.ids, bf16[512,1024]{1,0:T(8,128)(2,1)S(1)} %get-tuple-element.102.near_ref, bf16[512,1024]{1,0:T(8,128)(2,1)S(1)} %get-tuple-element.109.far_ref, bf16[2048,4096]{1,0:T(8,128)(2,1)S(1)} %copy-done), custom_call_target="tpu_custom_call" | custom-call | flops 536870912 | bytes 1048576 | tf_op jit(solution)/shard_map/pallas_call | solution.py:29
  70.5 1.6 %collective-permute-start.19 = (bf16[512,256]{1,0:T(8,128)(2,1)S(1)}, bf16[512,256]{1,0:T(8,128)(2,1)S(1)}, u32[]{:S(2)}, u32[]{:S(2)}) collective-permute-start(bf16[512,256]{1,0:T(8,128)(2,1)S(1)} %shard_map.93), channel_id=1, source_target_pairs={{0,1},{1,0},{2,3},{3,2},{4,5},{5,4},{6,7},{7,6},{8,9},{9,8},{10,11... | collective-permute-start | bytes 786440 | tf_op jit(solution)/shard_map/ppermute | solution.py:441
  72.6 5.1 %shard_map.92.own_ref = bf16[512,2048]{1,0:T(8,128)(2,1)S(1)} custom-call(s32[3]{0:T(128)S(1)} %pad_add_fusion.ids, bf16[512,1024]{1,0:T(8,128)(2,1)S(1)} %get-tuple-element.102.near_ref, bf16[512,1024]{1,0:T(8,128)(2,1)S(1)} %get-tuple-element.109.far_ref, bf16[2048,4096]{1,0:T(8,128)(2,1)S(1)} %copy-done), custom_call_target="tpu_custom_call" | custom-call | flops 4294967296 | bytes 8388608 | tf_op jit(solution)/shard_map/pallas_call | solution.py:29
  77.8 34.4 %collective-permute-done.22.rest_0_ = bf16[512,256]{1,0:T(8,128)(2,1)S(1)} collective-permute-done((bf16[512,256]{1,0:T(8,128)(2,1)S(1)}, bf16[512,256]{1,0:T(8,128)(2,1)S(1)}, u32[]{:S(2)}, u32[]{:S(2)}) %collective-permute-start.22) | collective-permute-done | bytes 262176 | tf_op jit(solution)/shard_map/ppermute | solution.py:441
  112.2 0.8 shard_map.96.rest_1_
  113.0 1.1 shard_map.97.rest_1_
  114.1 1.1 shard_map.98.rest_1_
  115.2 0.8 shard_map.99
  (34 shorter events, 1.5 us)
Async XLA Ops:
  0.8 11.0 %collective-permute-start = (bf16[16,1024]{1,0:T(8,128)(2,1)S(1)}, bf16[16,1024]{1,0:T(8,128)(2,1)S(1)}, u32[]{:S(2)}, u32[]{:S(2)}) collective-permute-start(bf16[16,1024]{1,0:T(8,128)(2,1)S(1)} %slice.3), channel_id=1, source_target_pairs={{0,2},{2,4},{4,6},{6,8},{8,10},{10,12},{12,14},{14,16},{16,18},{18... | collective-permute-start | bytes 98312 | tf_op jit(solution)/shard_map/ppermute | solution.py:344
  3.2 1.6 %copy-start.1 = (bf16[512,2048]{1,0:T(8,128)(2,1)S(1)}, bf16[512,2048]{1,0:T(8,128)(2,1)}, u32[]{:S(2)}) copy-start(bf16[512,2048]{1,0:T(8,128)(2,1)} %rest_4_.1) | copy-start | bytes 6291460
  4.8 1.2 %copy-start.2 = (bf16[512,1024]{1,0:T(8,128)(2,1)S(1)}, bf16[512,1024]{1,0:T(8,128)(2,1)}, u32[]{:S(2)}) copy-start(bf16[512,1024]{1,0:T(8,128)(2,1)} %rest_0_.1) | copy-start | bytes 3145732
  6.1 1.2 %copy-start.3 = (bf16[2,4,256,256]{3,2,1,0:T(8,128)(2,1)S(1)}, bf16[2,4,256,256]{3,2,1,0:T(8,128)(2,1)}, u32[]{:S(2)}) copy-start(bf16[2,4,256,256]{3,2,1,0:T(8,128)(2,1)} %rest_3_.1) | copy-start | bytes 3145732
  7.3 0.7 copy-start.4
  8.0 0.7 copy-start.5
  8.7 0.7 copy-start.6
  9.4 0.7 copy-start.7
  11.8 46.4 %copy-start = (bf16[2048,4096]{1,0:T(8,128)(2,1)S(1)}, bf16[2048,4096]{1,0:T(8,128)(2,1)}, u32[]{:S(2)}) copy-start(bf16[2048,4096]{1,0:T(8,128)(2,1)} %weight_ref.7) | copy-start | bytes 50331652
  14.1 5.0 %collective-permute-start.1 = (bf16[2,256,512]{2,1,0:T(8,128)(2,1)S(1)}, bf16[2,256,512]{2,1,0:T(8,128)(2,1)S(1)}, u32[]{:S(2)}, u32[]{:S(2)}) collective-permute-start(bf16[2,256,512]{2,1,0:T(8,128)(2,1)S(1)} %get-tuple-element.67), channel_id=1, source_target_pairs={{0,2},{2,0},{4,6},{6,4},{8,10},{10,8},{12,14},{14,12},{16,18},{18,... | collective-permute-start | bytes 1572872 | tf_op jit(solution)/shard_map/ppermute | solution.py:373
  16.7 2.4 %collective-permute-start.2 = (f32[8,128]{1,0:T(8,128)S(1)}, f32[8,128]{1,0:T(8,128)S(1)}, u32[]{:S(2)}, u32[]{:S(2)}) collective-permute-start(f32[8,128]{1,0:T(8,128)S(1)} %get-tuple-element.68.own_sums.rest_10_), channel_id=1, source_target_pairs={{0,2},{2,0},{4,6},{6,4},{8,10},{10,8},{12,14},{14,12},{16,18},{18,... | collective-permute-start | bytes 12296 | tf_op jit(solution)/shard_map/ppermute | solution.py:354
  19.9 7.5 %collective-permute-start.3 = (bf16[272,128]{1,0:T(8,128)(2,1)S(1)}, bf16[272,128]{1,0:T(8,128)(2,1)S(1)}, u32[]{:S(2)}, u32[]{:S(2)}) collective-permute-start(bf16[272,128]{1,0:T(8,128)(2,1)S(1)} %get-tuple-element.77), channel_id=1, source_target_pairs={{0,4},{2,6},{4,0},{6,2},{8,12},{10,14},{12,8},{14,10},{16,20},{18,... | collective-permute-start | bytes 208904 | tf_op jit(solution)/shard_map/ppermute | solution.py:341
  21.5 8.2 %collective-permute-start.4 = (bf16[272,128]{1,0:T(8,128)(2,1)S(1)}, bf16[272,128]{1,0:T(8,128)(2,1)S(1)}, u32[]{:S(2)}, u32[]{:S(2)}) collective-permute-start(bf16[272,128]{1,0:T(8,128)(2,1)S(1)} %get-tuple-element.78), channel_id=1, source_target_pairs={{0,8},{2,10},{4,12},{6,14},{8,0},{10,2},{12,4},{14,6},{16,24},{18,... | collective-permute-start | bytes 208904 | tf_op jit(solution)/shard_map/ppermute | solution.py:341
  23.1 9.8 %collective-permute-start.5 = (bf16[272,128]{1,0:T(8,128)(2,1)S(1)}, bf16[272,128]{1,0:T(8,128)(2,1)S(1)}, u32[]{:S(2)}, u32[]{:S(2)}) collective-permute-start(bf16[272,128]{1,0:T(8,128)(2,1)S(1)} %get-tuple-element.79), channel_id=1, source_target_pairs={{0,12},{2,14},{4,8},{6,10},{8,4},{10,6},{12,0},{14,2},{16,28},{18,... | collective-permute-start | bytes 208904 | tf_op jit(solution)/shard_map/ppermute | solution.py:341
  23.5 9.5 %collective-permute-start.6 = (bf16[272,128]{1,0:T(8,128)(2,1)S(1)}, bf16[272,128]{1,0:T(8,128)(2,1)S(1)}, u32[]{:S(2)}, u32[]{:S(2)}) collective-permute-start(bf16[272,128]{1,0:T(8,128)(2,1)S(1)} %get-tuple-element.80), channel_id=1, source_target_pairs={{0,16},{2,18},{4,20},{6,22},{8,24},{10,26},{12,28},{14,30},{16,0},... | collective-permute-start | bytes 208904 | tf_op jit(solution)/shard_map/ppermute | solution.py:341
  26.0 11.3 %collective-permute-start.7 = (bf16[272,128]{1,0:T(8,128)(2,1)S(1)}, bf16[272,128]{1,0:T(8,128)(2,1)S(1)}, u32[]{:S(2)}, u32[]{:S(2)}) collective-permute-start(bf16[272,128]{1,0:T(8,128)(2,1)S(1)} %get-tuple-element.81), channel_id=1, source_target_pairs={{0,20},{2,22},{4,16},{6,18},{8,28},{10,30},{12,24},{14,26},{16,4},... | collective-permute-start | bytes 208904 | tf_op jit(solution)/shard_map/ppermute | solution.py:341
  27.4 9.9 %collective-permute-start.8 = (bf16[272,128]{1,0:T(8,128)(2,1)S(1)}, bf16[272,128]{1,0:T(8,128)(2,1)S(1)}, u32[]{:S(2)}, u32[]{:S(2)}) collective-permute-start(bf16[272,128]{1,0:T(8,128)(2,1)S(1)} %get-tuple-element.82), channel_id=1, source_target_pairs={{0,24},{2,26},{4,28},{6,30},{8,16},{10,18},{12,20},{14,22},{16,8},... | collective-permute-start | bytes 208904 | tf_op jit(solution)/shard_map/ppermute | solution.py:341
  29.7 7.6 %collective-permute-start.9 = (bf16[272,128]{1,0:T(8,128)(2,1)S(1)}, bf16[272,128]{1,0:T(8,128)(2,1)S(1)}, u32[]{:S(2)}, u32[]{:S(2)}) collective-permute-start(bf16[272,128]{1,0:T(8,128)(2,1)S(1)} %get-tuple-element.83), channel_id=1, source_target_pairs={{0,28},{2,30},{4,24},{6,26},{8,20},{10,22},{12,16},{14,18},{16,12}... | collective-permute-start | bytes 208904 | tf_op jit(solution)/shard_map/ppermute | solution.py:341
  38.1 8.3 %collective-permute-start.10 = (bf16[272,128]{1,0:T(8,128)(2,1)S(1)}, bf16[272,128]{1,0:T(8,128)(2,1)S(1)}, u32[]{:S(2)}, u32[]{:S(2)}) collective-permute-start(bf16[272,128]{1,0:T(8,128)(2,1)S(1)} %get-tuple-element.91), channel_id=1, source_target_pairs={{0,4},{2,6},{4,0},{6,2},{8,12},{10,14},{12,8},{14,10},{16,20},{18,... | collective-permute-start | bytes 208904 | tf_op jit(solution)/shard_map/ppermute | solution.py:341
  39.4 9.3 %collective-permute-start.11 = (bf16[272,128]{1,0:T(8,128)(2,1)S(1)}, bf16[272,128]{1,0:T(8,128)(2,1)S(1)}, u32[]{:S(2)}, u32[]{:S(2)}) collective-permute-start(bf16[272,128]{1,0:T(8,128)(2,1)S(1)} %get-tuple-element.92), channel_id=1, source_target_pairs={{0,8},{2,10},{4,12},{6,14},{8,0},{10,2},{12,4},{14,6},{16,24},{18,... | collective-permute-start | bytes 208904 | tf_op jit(solution)/shard_map/ppermute | solution.py:341
  42.6 9.8 %collective-permute-start.12 = (bf16[272,128]{1,0:T(8,128)(2,1)S(1)}, bf16[272,128]{1,0:T(8,128)(2,1)S(1)}, u32[]{:S(2)}, u32[]{:S(2)}) collective-permute-start(bf16[272,128]{1,0:T(8,128)(2,1)S(1)} %get-tuple-element.93), channel_id=1, source_target_pairs={{0,12},{2,14},{4,8},{6,10},{8,4},{10,6},{12,0},{14,2},{16,28},{18,... | collective-permute-start | bytes 208904 | tf_op jit(solution)/shard_map/ppermute | solution.py:341
  42.9 10.4 %collective-permute-start.13 = (bf16[272,128]{1,0:T(8,128)(2,1)S(1)}, bf16[272,128]{1,0:T(8,128)(2,1)S(1)}, u32[]{:S(2)}, u32[]{:S(2)}) collective-permute-start(bf16[272,128]{1,0:T(8,128)(2,1)S(1)} %get-tuple-element.94), channel_id=1, source_target_pairs={{0,16},{2,18},{4,20},{6,22},{8,24},{10,26},{12,28},{14,30},{16,0},... | collective-permute-start | bytes 208904 | tf_op jit(solution)/shard_map/ppermute | solution.py:341
  45.7 10.9 %collective-permute-start.14 = (bf16[272,128]{1,0:T(8,128)(2,1)S(1)}, bf16[272,128]{1,0:T(8,128)(2,1)S(1)}, u32[]{:S(2)}, u32[]{:S(2)}) collective-permute-start(bf16[272,128]{1,0:T(8,128)(2,1)S(1)} %get-tuple-element.95), channel_id=1, source_target_pairs={{0,20},{2,22},{4,16},{6,18},{8,28},{10,30},{12,24},{14,26},{16,4},... | collective-permute-start | bytes 208904 | tf_op jit(solution)/shard_map/ppermute | solution.py:341
  46.4 10.2 %collective-permute-start.15 = (bf16[272,128]{1,0:T(8,128)(2,1)S(1)}, bf16[272,128]{1,0:T(8,128)(2,1)S(1)}, u32[]{:S(2)}, u32[]{:S(2)}) collective-permute-start(bf16[272,128]{1,0:T(8,128)(2,1)S(1)} %get-tuple-element.96), channel_id=1, source_target_pairs={{0,24},{2,26},{4,28},{6,30},{8,16},{10,18},{12,20},{14,22},{16,8},... | collective-permute-start | bytes 208904 | tf_op jit(solution)/shard_map/ppermute | solution.py:341
  48.7 7.9 %collective-permute-start.16 = (bf16[272,128]{1,0:T(8,128)(2,1)S(1)}, bf16[272,128]{1,0:T(8,128)(2,1)S(1)}, u32[]{:S(2)}, u32[]{:S(2)}) collective-permute-start(bf16[272,128]{1,0:T(8,128)(2,1)S(1)} %get-tuple-element.97), channel_id=1, source_target_pairs={{0,28},{2,30},{4,24},{6,26},{8,20},{10,22},{12,16},{14,18},{16,12}... | collective-permute-start | bytes 208904 | tf_op jit(solution)/shard_map/ppermute | solution.py:341
  57.6 2.6 %collective-permute-start.17 = (bf16[2,256,512]{2,1,0:T(8,128)(2,1)S(1)}, bf16[2,256,512]{2,1,0:T(8,128)(2,1)S(1)}, u32[]{:S(2)}, u32[]{:S(2)}) collective-permute-start(bf16[2,256,512]{2,1,0:T(8,128)(2,1)S(1)} %get-tuple-element.105), channel_id=1, source_target_pairs={{0,2},{2,0},{4,6},{6,4},{8,10},{10,8},{12,14},{14,12},{16,18},{18,... | collective-permute-start | bytes 1572872 | tf_op jit(solution)/shard_map/ppermute | solution.py:406
  57.6 2.5 %collective-permute-start.18 = (f32[8,128]{1,0:T(8,128)S(1)}, f32[8,128]{1,0:T(8,128)S(1)}, u32[]{:S(2)}, u32[]{:S(2)}) collective-permute-start(f32[8,128]{1,0:T(8,128)S(1)} %get-tuple-element.106), channel_id=1, source_target_pairs={{0,2},{2,0},{4,6},{6,4},{8,10},{10,8},{12,14},{14,12},{16,18},{18,... | collective-permute-start | bytes 12296 | tf_op jit(solution)/shard_map/ppermute | solution.py:407
  64.5 48.5 %collective-permute-start.21 = (bf16[512,768]{1,0:T(8,128)(2,1)S(1)}, bf16[512,768]{1,0:T(8,128)(2,1)S(1)}, u32[]{:S(2)}, u32[]{:S(2)}) collective-permute-start(bf16[512,768]{1,0:T(8,128)(2,1)S(1)} %shard_map.95), channel_id=1, source_target_pairs={{0,1},{1,0},{2,3},{3,2},{4,5},{5,4},{6,7},{7,6},{8,9},{9,8},{10,11... | collective-permute-start | bytes 2359304 | tf_op jit(solution)/shard_map/ppermute | solution.py:441
  68.7 45.4 %collective-permute-start.20 = (bf16[512,768]{1,0:T(8,128)(2,1)S(1)}, bf16[512,768]{1,0:T(8,128)(2,1)S(1)}, u32[]{:S(2)}, u32[]{:S(2)}) collective-permute-start(bf16[512,768]{1,0:T(8,128)(2,1)S(1)} %shard_map.94), channel_id=1, source_target_pairs={{0,1},{1,0},{2,3},{3,2},{4,5},{5,4},{6,7},{7,6},{8,9},{9,8},{10,11... | collective-permute-start | bytes 2359304 | tf_op jit(solution)/shard_map/ppermute | solution.py:441
  70.5 44.7 %collective-permute-start.19 = (bf16[512,256]{1,0:T(8,128)(2,1)S(1)}, bf16[512,256]{1,0:T(8,128)(2,1)S(1)}, u32[]{:S(2)}, u32[]{:S(2)}) collective-permute-start(bf16[512,256]{1,0:T(8,128)(2,1)S(1)} %shard_map.93), channel_id=1, source_target_pairs={{0,1},{1,0},{2,3},{3,2},{4,5},{5,4},{6,7},{7,6},{8,9},{9,8},{10,11... | collective-permute-start | bytes 786440 | tf_op jit(solution)/shard_map/ppermute | solution.py:441
  72.1 40.1 %collective-permute-start.22 = (bf16[512,256]{1,0:T(8,128)(2,1)S(1)}, bf16[512,256]{1,0:T(8,128)(2,1)S(1)}, u32[]{:S(2)}, u32[]{:S(2)}) collective-permute-start(bf16[512,256]{1,0:T(8,128)(2,1)S(1)} %get-tuple-element.110), channel_id=1, source_target_pairs={{0,1},{1,0},{2,3},{3,2},{4,5},{5,4},{6,7},{7,6},{8,9},{9,8},{10,11... | collective-permute-start | bytes 786440 | tf_op jit(solution)/shard_map/ppermute | solution.py:441
